TPU v7x, 32 devices: a whole 2x2x4 slice. The times are simulated.
32 devices in a mesh: tile: 8 (over z, y), depth: 4 (over x, core).
Axes of the slice: x: 2, y: 2, z: 4, core: 2. Of those that a mesh axis runs over, the one named last changes fastest.
Arguments:
- positions: float32 [3, 16384], P(None, 'tile'), may hold values from -4 to 4
- log_scales: float32 [3, 16384], P(None, 'tile'), may hold values from -2 to 0
- opacity_logits: float32 [1, 16384], P(None, 'tile'), may hold values from -3 to 1.5
- colors: float32 [3, 16384], P(None, 'tile'), may hold values from 0 to 1
- first_moment: float32 [10, 16384], P(None, 'tile'), may hold values from -3 to 3
- second_moment: float32 [10, 16384], P(None, 'tile'), may hold values from 0.01 to 1
- cameras: float32 [4, 2, 4], replicated, may hold values from -6.4 to 6.4
- background: float32 [3], replicated, may hold values from 0 to 1
- target: float32 [32, 3, 1024], P('tile'), may hold values from 0 to 1
- tile_view: int32 [32], P('tile'), may hold values from 0 to 3
- tile_length: int32 [32], P('tile'), may hold values from 128 to 512
- list_owner: int32 [4, 32, 128, 1], P('depth', 'tile'), may hold values from 0 to 7; in each aligned block of 512 rows (0 to 511, 512 to 1023, ..., all dimensions but the last counted through in order) at most 160 rows name the same one
- list_row: int32 [4, 32, 128], P('depth', 'tile'), may hold values from 0 to 2047
Outputs:
- image: float32 [32, 3, 1024], P('tile')
- new_params: float32 [10, 16384], P(None, 'tile')
- new_first: float32 [10, 16384], P(None, 'tile')
- new_second: float32 [10, 16384], P(None, 'tile')
Inputs may be any that keep to these rules, and one draw needn't show every extreme that they name: `list_owner`: within the entries of one device's block (one depth slab of the tiles of one tile index), no owner is named more than 160 times, a bound that some block reaches.
All inputs are finite; a program needn't handle non-finite values.
Results may differ from a plain program's by a relative error of at most 0.00008.
Values sent between devices are 32-bit elements; how exact they have to be, the bound alone decides.
A program may use at most 64 MiB of HBM per device.

v0:
```python
import jax
import jax.numpy as jnp
from jax import lax
from jax.sharding import PartitionSpec as P

TILE_SIDE = 32


def project(params, cams):
    position = params[0:3]
    variance = jnp.exp(2.0 * params[3:6])
    first_row = cams[:, 0, 0:3].T
    second_row = cams[:, 1, 0:3].T
    center_x = jnp.sum(first_row * position, axis=0) + cams[:, 0, 3] + 0.5 * TILE_SIDE
    center_y = jnp.sum(second_row * position, axis=0) + cams[:, 1, 3] + 0.5 * TILE_SIDE
    cov_xx = jnp.sum(first_row * first_row * variance, axis=0) + 0.3
    cov_xy = jnp.sum(first_row * second_row * variance, axis=0)
    cov_yy = jnp.sum(second_row * second_row * variance, axis=0) + 0.3
    determinant = cov_xx * cov_yy - cov_xy * cov_xy
    return jnp.stack(
        [
            center_x,
            center_y,
            cov_yy / determinant,
            -cov_xy / determinant,
            cov_xx / determinant,
            jax.nn.sigmoid(params[6]),
            params[7],
            params[8],
            params[9],
        ]
    )


def coverage(screen, alive, pixels):
    pixel = jnp.arange(pixels, dtype=jnp.int32)
    pixel_x = (pixel % TILE_SIDE).astype(jnp.float32) + 0.5
    pixel_y = (pixel // TILE_SIDE).astype(jnp.float32) + 0.5
    offset_x = pixel_x[:, None] - screen[0][None, :]
    offset_y = pixel_y[:, None] - screen[1][None, :]
    quadric = (
        screen[2][None, :] * offset_x * offset_x
        + 2.0 * screen[3][None, :] * offset_x * offset_y
        + screen[4][None, :] * offset_y * offset_y
    )
    falloff = jnp.exp(-0.5 * quadric)
    alpha = screen[5][None, :] * falloff * alive[None, :]
    return (offset_x, offset_y, falloff, alpha)


def running_sum(values, triangle):
    rows = values.shape[0]
    width = triangle.shape[0]
    blocks = values.reshape(rows, values.shape[1] // width, width)
    inner = jnp.einsum("pbk,kj->pbj", blocks, triangle, precision=lax.Precision.HIGHEST)
    sums = jnp.sum(blocks, axis=2)
    lead = jnp.cumsum(sums, axis=1) - sums
    return (inner + lead[:, :, None]).reshape(rows, values.shape[1])


def adam_update(param, first, second, gradient):
    new_first = 0.9 * first + 0.1 * gradient
    new_second = 0.999 * second + 0.001 * gradient * gradient
    corrected = new_first / (1.0 - 0.9**10) / (jnp.sqrt(new_second / (1.0 - 0.999**10)) + 1e-08)
    return (param - 0.05 * corrected, new_first, new_second)


def body(
    positions,
    log_scales,
    opacity_logits,
    colors,
    first_moment,
    second_moment,
    cameras,
    background,
    target,
    tile_view,
    tile_length,
    list_owner,
    list_row,
):
    tiles_here = target.shape[0]
    pixels = target.shape[2]
    slab = list_row.shape[2]
    owner_count = lax.axis_size("tile")
    depth_count = lax.axis_size("depth")
    depth_index = lax.axis_index("depth")
    capacity = max(2, 5 * tiles_here * slab // (2 * owner_count))
    highest = lax.Precision.HIGHEST
    params = jnp.concatenate([positions, log_scales, opacity_logits, colors], axis=0)
    owner = list_owner.reshape(-1)
    wanted = list_row.reshape(-1)
    viewed = jnp.repeat(tile_view, slab)
    onehot = (owner[:, None] == jnp.arange(owner_count, dtype=jnp.int32)[None, :]).astype(jnp.int32)
    rank = jnp.sum((jnp.cumsum(onehot, axis=0) - onehot) * onehot, axis=1)
    slot = owner * capacity + rank
    request = (
        jnp.zeros((2, owner_count * capacity), jnp.int32)
        .at[:, slot]
        .set(jnp.stack([wanted, viewed]))
    )
    request = request.reshape(2, owner_count, capacity)
    received = lax.all_to_all(request, "tile", split_axis=1, concat_axis=1, tiled=True)
    rows_in = received[0].reshape(-1)
    views_in = received[1].reshape(-1)
    screen = project(params[:, rows_in], cameras[views_in])
    screen = screen.reshape(9, received.shape[1], received.shape[2])
    fetched = lax.all_to_all(screen, "tile", split_axis=1, concat_axis=1, tiled=True)
    entry = fetched.reshape(9, -1)[:, slot].reshape(9, tiles_here, slab).transpose(1, 0, 2)
    order = jnp.arange(slab, dtype=jnp.int32)
    strict = (order[:, None] < order[None, :]).astype(jnp.float32)
    inclusive = (order[:, None] <= order[None, :]).astype(jnp.float32)

    def forward(args):
        screen, alive = args
        offset_x, offset_y, falloff, alpha = coverage(screen, alive, pixels)
        leak = jnp.log1p(-alpha)
        before = running_sum(leak, strict)
        weight = alpha * jnp.exp(before)
        color = jnp.einsum("ck,pk->cp", screen[6:9], weight, precision=highest)
        return (jnp.sum(leak, axis=1), color)

    def backward(args):
        screen, alive, start_log, start_color, whole, miss = args
        offset_x, offset_y, falloff, alpha = coverage(screen, alive, pixels)
        leak = jnp.log1p(-alpha)
        local = running_sum(leak, strict)
        carried = jnp.exp(start_log)[:, None]
        inside = jnp.exp(local)
        trans = carried * inside
        weight = alpha * trans
        local_weight = alpha * inside
        d_alpha = jnp.zeros_like(alpha)
        for channel in range(3):
            shade = screen[6 + channel][None, :]
            upto = running_sum(local_weight * shade, inclusive)
            behind = whole[channel][:, None] - start_color[channel][:, None] - carried * upto
            d_alpha = d_alpha + miss[channel][:, None] * (trans * shade - behind / (1.0 - alpha))
        d_color = jnp.einsum("cp,pk->ck", miss, weight, precision=highest)
        d_quad = d_alpha * (-0.5 * alpha)
        d_opacity = jnp.sum(d_alpha * falloff * alive[None, :], axis=0)
        d_center_x = jnp.sum(
            d_quad * -2.0 * (screen[2][None, :] * offset_x + screen[3][None, :] * offset_y), axis=0
        )
        d_center_y = jnp.sum(
            d_quad * -2.0 * (screen[3][None, :] * offset_x + screen[4][None, :] * offset_y), axis=0
        )
        d_conic_a = jnp.sum(d_quad * offset_x * offset_x, axis=0)
        d_conic_b = jnp.sum(d_quad * 2.0 * offset_x * offset_y, axis=0)
        d_conic_c = jnp.sum(d_quad * offset_y * offset_y, axis=0)
        return jnp.concatenate(
            [
                jnp.stack([d_center_x, d_center_y, d_conic_a, d_conic_b, d_conic_c, d_opacity]),
                d_color,
            ],
            axis=0,
        )

    quarter = tiles_here // depth_count
    whole_entry = lax.all_to_all(entry, "depth", split_axis=0, concat_axis=2, tiled=True)
    first_tile = depth_index * quarter
    own_length = lax.dynamic_slice_in_dim(tile_length, first_tile, quarter, 0)
    full_place = jnp.arange(slab * depth_count, dtype=jnp.int32)
    own_live = (full_place[None, :] < own_length[:, None]).astype(jnp.float32)
    own_log, own_color = lax.map(forward, (whole_entry, own_live))
    own_image = own_color + jnp.exp(own_log)[:, None, :] * background[None, :, None]
    own_error = own_image - lax.dynamic_slice_in_dim(target, first_tile, quarter, 0)
    zero_log = jnp.zeros_like(own_log)
    zero_color = jnp.zeros_like(own_color)
    own_grad = lax.map(
        backward, (whole_entry, own_live, zero_log, zero_color, own_image, own_error)
    )
    entry_grad = lax.all_to_all(own_grad, "depth", split_axis=2, concat_axis=0, tiled=True)
    image = lax.all_gather(own_image, "depth", axis=0, tiled=True)
    flat_grad = entry_grad.transpose(1, 0, 2).reshape(9, -1)
    outgoing = jnp.zeros((9, owner_count * capacity), jnp.float32).at[:, slot].set(flat_grad)
    outgoing = outgoing.reshape(9, owner_count, capacity)
    incoming = lax.all_to_all(outgoing, "tile", split_axis=1, concat_axis=1, tiled=True)
    rows_in = received[0].reshape(-1)
    views_in = received[1].reshape(-1)
    chosen_cams = cameras[views_in]
    unused, pullback = jax.vjp(lambda chosen: project(chosen, chosen_cams), params[:, rows_in])
    (slot_grad,) = pullback(incoming.reshape(9, -1))
    gradient = jnp.zeros_like(params).at[:, rows_in].add(slot_grad)
    gradient = lax.psum(gradient, "depth")
    new_params, new_first, new_second = adam_update(params, first_moment, second_moment, gradient)
    return (image, new_params, new_first, new_second)


def solution(mesh):
    placed = (
        P(None, "tile"),
        P(None, "tile"),
        P(None, "tile"),
        P(None, "tile"),
        P(None, "tile"),
        P(None, "tile"),
        P(),
        P(),
        P("tile", None, None),
        P("tile"),
        P("tile"),
        P("depth", "tile", None, None),
        P("depth", "tile", None),
    )
    return jax.shard_map(
        body,
        mesh=mesh,
        in_specs=placed,
        out_specs=(P("tile", None, None), P(None, "tile"), P(None, "tile"), P(None, "tile")),
        check_vma=False,
    )
```

profile of v0, /device:TPU:0, one launch (start us, length us, event | category | flops | bytes accessed | tf_op | source)
XLA Modules:
  0.0 199.4 jit_solution(7363935695881023951)
XLA Ops:
  7.9 1.1 reduce-window.6
  12.3 1.9 scatter_custom_fusion
  15.2 7.3 %all-to-all-start = ((s32[2,8,160]{2,0,1:T(2,128)}), s32[2,8,160]{2,0,1:T(2,128)S(1)}, u32[]{:S(2)}, u32[]{:S(2)}) async-start(s32[2,8,160]{2,0,1:T(2,128)} %copy.152), calls=%async_computation | async-start | bytes 32768 | tf_op jit(solution)/shard_map/all_to_all | solution.py:104
  24.3 4.7 %all-to-all-done = s32[2,8,160]{2,0,1:T(2,128)S(1)} async-done(((s32[2,8,160]{2,0,1:T(2,128)}), s32[2,8,160]{2,0,1:T(2,128)S(1)}, u32[]{:S(2)}, u32[]{:S(2)}) %all-to-all-start) | async-done | bytes 10272 | tf_op jit(solution)/shard_map/all_to_all | solution.py:104
  29.2 4.3 %gather_fusion = f32[1280,2,4]{2,1,0:T(2,128)S(1)} fusion(f32[4,2,4]{2,1,0:T(2,128)S(1)} %copy-done.1, s32[2048]{0:T(1024)S(1)} %pad_clamp_fusion.1), kind=kCustom, calls=%fused_computation | custom fusion | bytes 87040 | tf_op jit(solution)/shard_map/gather | solution.py:107
  33.6 1.8 fusion.84
  35.3 36.3 %slice_reduce_fusion = (f32[1280]{0:T(1024)S(1)}, f32[1280]{0:T(1024)S(1)}) fusion(f32[1280,2,4]{2,1,0:T(2,128)S(1)} %gather_fusion), kind=kLoop, calls=%fused_computation.71 | loop fusion | bytes 20480 | tf_op jit(solution)/shard_map/slice | solution.py:15
  71.6 1.3 copy.189
  73.4 2.4 %gather_fusion.1 = f32[1280,10]{1,0:T(8,128)S(1)} fusion(f32[10,2048]{0,1:T(8,128)S(1)} %copy.154, s32[2048]{0:T(1024)S(1)} %pad_clamp_fusion), kind=kCustom, calls=%fused_computation.1 | custom fusion | bytes 107520 | tf_op jit(solution)/shard_map/gather | solution.py:107
  78.0 3.5 %all-to-all-start.1 = ((f32[8,1,1440]{2,1,0:T(1,128)}), f32[8,1,1440]{2,1,0:T(1,128)S(1)}, u32[]{:S(2)}, u32[]{:S(2)}) async-start(f32[8,1,1440]{2,1,0:T(1,128)} %reshape.1452), calls=%async_computation.1 | async-start | bytes 98304 | tf_op jit(solution)/shard_map/all_to_all | solution.py:109
  82.2 5.9 %all-to-all-done.1 = f32[8,1,1440]{2,1,0:T(1,128)S(1)} async-done(((f32[8,1,1440]{2,1,0:T(1,128)}), f32[8,1,1440]{2,1,0:T(1,128)S(1)}, u32[]{:S(2)}, u32[]{:S(2)}) %all-to-all-start.1) | async-done | bytes 46112 | tf_op jit(solution)/shard_map/all_to_all | solution.py:109
  89.7 1.0 gather_fusion.2
  91.5 3.3 %all-to-all-start.2 = ((f32[4,9,128]{2,1,0:T(8,128)}), f32[4,9,128]{2,1,0:T(8,128)S(1)}, u32[]{:S(2)}, u32[]{:S(2)}) async-start(f32[4,9,128]{2,1,0:T(8,128)} %bitcast.21), calls=%async_computation.2 | async-start | bytes 65536 | tf_op jit(solution)/shard_map/all_to_all | solution.py:161
  95.5 3.2 %all-to-all-done.2 = f32[4,9,128]{2,1,0:T(8,128)S(1)} async-done(((f32[4,9,128]{2,1,0:T(8,128)}), f32[4,9,128]{2,1,0:T(8,128)S(1)}, u32[]{:S(2)}, u32[]{:S(2)}) %all-to-all-start.2) | async-done | bytes 18464 | tf_op jit(solution)/shard_map/all_to_all | solution.py:161
  98.7 2.0 fusion.28
  100.8 5.9 %multiply_reduce_fusion.3 = (f32[1024,4]{0,1:T(4,128)S(1)}, f32[1024,4]{0,1:T(4,128)S(1)}, f32[1024,4]{0,1:T(4,128)S(1)}, f32[1024,4,128]{0,2,1:T(8,128)S(1)}, f32[1024,4,128]{0,2,1:T(8,128)}) fusion(f32[4,128]{1,0:T(4,128)S(1)} %bitcast.208, f32[4,128]{1,0:T(4,128)S(1)} %bitcast.188, f32[4,128]{1,0:T(4,128)S(1)} %bitcast.185, f32[1024,4]{0,1:T(4,128)S(1)} %sub.316, ...), kind=kOutput, calls=%fused_computation.60 | convolution fusion | flops 823660544 | bytes 4288512 | tf_op jit(solution)/shard_map/while/body/eval_jaxpr/pbk,kj->pbj/dot_general | solution.py:55
  106.7 2.9 %fusion.24 = f32[1024,4,128]{0,2,1:T(8,128)} fusion(f32[1024,4,128]{0,2,1:T(8,128)S(1)} %get-tuple-element.96, f32[4,128]{1,0:T(4,128)S(1)} %bitcast.189), kind=kOutput, calls=%fused_computation.58 | convolution fusion | flops 805847040 | bytes 4196352 | tf_op jit(solution)/shard_map/while/body/eval_jaxpr/pbk,kj->pbj/dot_general | solution.py:55
  109.6 2.9 %fusion.22 = f32[1024,4,128]{0,2,1:T(8,128)} fusion(f32[1024,4,128]{0,2,1:T(8,128)S(1)} %get-tuple-element.96, f32[4,128]{1,0:T(4,128)S(1)} %bitcast.186), kind=kOutput, calls=%fused_computation.55 | convolution fusion | flops 805847040 | bytes 4196352 | tf_op jit(solution)/shard_map/while/body/eval_jaxpr/pbk,kj->pbj/dot_general | solution.py:55
  112.5 1.9 fusion.14
  114.4 1.1 copy_subtract_fusion
  115.5 1.8 fusion.56
  117.5 6.2 %multiply_multiply_fusion = (f32[1024,4,128]{0,2,1:T(8,128)S(1)}, f32[1024,4,128]{0,2,1:T(8,128)S(1)}) fusion(f32[4,128]{1,0:T(4,128)S(1)} %fusion.74, f32[4,128]{1,0:T(4,128)S(1)} %bitcast.168, f32[4,128]{1,0:T(4,128)S(1)} %bitcast.173, f32[1024]{0:T(1024)S(1)} %get-tuple-element.136, f32[4,128]{1,0:T(4,128)S(1)} %broadcast_multiply_fusion.1, ...), kind=kOutput, calls=%fused_computation.49 | convolution fusion | flops 825245696 | bytes 12701696 | tf_op jit(solution)/shard_map/while/body/eval_jaxpr/pbk,kj->pbj/dot_general | solution.py:55
  123.7 3.8 %fusion.3 = (f32[4,128]{1,0:T(4,128)S(1)}, f32[4,128]{1,0:T(4,128)S(1)}, f32[4,128]{1,0:T(4,128)S(1)}, f32[4,128]{1,0:T(4,128)S(1)}, f32[4,128]{1,0:T(4,128)S(1)}, /*index=5*/f32[4,128]{1,0:T(4,128)S(1)}) fusion(f32[1024,4,128]{0,2,1:T(8,128)S(1)} %get-tuple-element.131, f32[4,128]{1,0:T(4,128)S(1)} %bitcast.162, f32[4,128]{1,0:T(4,128)S(1)} %bitcast.169, ...), kind=kLoop, calls=%fused_computation.29 | loop fusion | flops 17298432 | bytes 4229120 | tf_op jit(solution)/shard_map/while/body/eval_jaxpr/reduce_sum | solution.py:146
  127.9 1.3 reduce.41
  129.4 6.2 %all_to_all.48 = f32[4,1,1152]{2,1,0:T(1,128)S(1)} all-to-all(f32[4,1,1152]{2,1,0:T(1,128)S(1)} %reshape.1454), channel_id=1, replica_groups=mesh['tile'=8,'depth'=4] {'depth'}, dimensions={0} | all-to-all | bytes 36864 | tf_op jit(solution)/shard_map/all_to_all | solution.py:174
  137.0 1.9 scatter_custom_fusion.1
  139.3 9.2 %all_to_all.49 = f32[8,1,1440]{2,1,0:T(1,128)S(1)} all-to-all(f32[8,1,1440]{2,1,0:T(1,128)S(1)} %reshape.1456), channel_id=1, replica_groups=mesh['tile'=8,'depth'=4] {'tile'}, dimensions={0} | all-to-all | bytes 92160 | tf_op jit(solution)/shard_map/all_to_all | solution.py:179
  150.8 9.2 %scatter_custom_fusion.2 = f32[10,2048]{0,1:T(8,128)S(1)} fusion(s32[1280]{0:T(1024)S(1)} %fusion.60, f32[1280,10]{1,0:T(8,128)S(1)} %copy.178, f32[]{:T(128)} %constant.132.clone.1), kind=kCustom, calls=%fused_computation.73 | custom fusion | flops 12800 | bytes 81924 | tf_op jit(solution)/shard_map/scatter-add | solution.py:185
  160.0 1.0 copy.179
  161.0 5.2 %all-gather.1 = f32[4,3,1024]{2,1,0:T(4,128)S(1)} all-gather(f32[1,3,1024]{2,1,0:T(4,128)S(1)} %get-tuple-element.130), channel_id=2, replica_groups=mesh['tile'=8,'depth'=4] {'depth'}, dimensions={0}, use_global_device_ids=true | all-gather | bytes 61440 | tf_op jit(solution)/shard_map/all_gather | solution.py:175
  166.8 23.9 %all-reduce.8.cloned.1.call-done = f32[10,2048]{1,0:T(8,128)} async-done(((f32[10,2048]{1,0:T(8,128)}), f32[10,2048]{1,0:T(8,128)}) %all-reduce.8.cloned.1.call-update) | async-done | bytes 81936 | tf_op jit(solution)/shard_map/psum | solution.py:186
  190.8 1.7 multiply_subtract_fusion
  (119 shorter events, 18.8 us)
Async XLA Ops:
  7.2 15.3 %copy-start = (f32[4,3,1024]{2,0,1:T(4,128)S(1)}, f32[4,3,1024]{2,0,1:T(4,128)}, u32[]{:S(2)}) copy-start(f32[4,3,1024]{2,0,1:T(4,128)} %param.21) | copy-start | bytes 147460
  7.2 16.6 %copy-start.9 = (s32[4]{0:T(128)S(1)}, s32[4]{0:T(128)}, u32[]{:S(2)}) copy-start(s32[4]{0:T(128)} %param.23) | copy-start | bytes 52
  7.2 22.0 %copy-start.1 = (f32[4,2,4]{2,1,0:T(2,128)S(1)}, f32[4,2,4]{2,1,0:T(2,128)}, u32[]{:S(2)}) copy-start(f32[4,2,4]{2,1,0:T(2,128)} %param.19) | copy-start | bytes 388
  15.2 13.9 %all-to-all-start = ((s32[2,8,160]{2,0,1:T(2,128)}), s32[2,8,160]{2,0,1:T(2,128)S(1)}, u32[]{:S(2)}, u32[]{:S(2)}) async-start(s32[2,8,160]{2,0,1:T(2,128)} %copy.152), calls=%async_computation | async-start | bytes 32768 | tf_op jit(solution)/shard_map/all_to_all | solution.py:104
  78.0 10.1 %all-to-all-start.1 = ((f32[8,1,1440]{2,1,0:T(1,128)}), f32[8,1,1440]{2,1,0:T(1,128)S(1)}, u32[]{:S(2)}, u32[]{:S(2)}) async-start(f32[8,1,1440]{2,1,0:T(1,128)} %reshape.1452), calls=%async_computation.1 | async-start | bytes 98304 | tf_op jit(solution)/shard_map/all_to_all | solution.py:109
  91.5 7.2 %all-to-all-start.2 = ((f32[4,9,128]{2,1,0:T(8,128)}), f32[4,9,128]{2,1,0:T(8,128)S(1)}, u32[]{:S(2)}, u32[]{:S(2)}) async-start(f32[4,9,128]{2,1,0:T(8,128)} %bitcast.21), calls=%async_computation.2 | async-start | bytes 65536 | tf_op jit(solution)/shard_map/all_to_all | solution.py:161
  94.8 96.0 %all-reduce.8.cloned.1.call-start = ((), (), s32[]{:S(2)}) async-start(), calls=%async_computation.5 | async-start | bytes 262144 | tf_op jit(solution)/shard_map/psum | solution.py:186
  109.6 4.8 %copy-start.8 = (f32[3]{0:T(128)S(1)}, f32[3]{0:T(128)}, u32[]{:S(2)}) copy-start(f32[3]{0:T(128)} %param.20) | copy-start | bytes 40
  149.3 41.5 %copy-start.2 = (f32[3,2048]{1,0:T(4,128)S(1)}, f32[3,2048]{1,0:T(4,128)}, u32[]{:S(2)}) copy-start(f32[3,2048]{1,0:T(4,128)} %param.16) | copy-start | bytes 73732
  149.3 41.5 %copy-start.3 = (f32[3,2048]{1,0:T(4,128)S(1)}, f32[3,2048]{1,0:T(4,128)}, u32[]{:S(2)}) copy-start(f32[3,2048]{1,0:T(4,128)} %param.14) | copy-start | bytes 73732
  149.3 41.4 %copy-start.4 = (f32[3,2048]{1,0:T(4,128)S(1)}, f32[3,2048]{1,0:T(4,128)}, u32[]{:S(2)}) copy-start(f32[3,2048]{1,0:T(4,128)} %param.13) | copy-start | bytes 73732
  149.3 41.4 %copy-start.5 = (f32[10,2048]{1,0:T(8,128)S(1)}, f32[10,2048]{1,0:T(8,128)}, u32[]{:S(2)}) copy-start(f32[10,2048]{1,0:T(8,128)} %param.17) | copy-start | bytes 245764
  149.3 41.4 %copy-start.6 = (f32[10,2048]{1,0:T(8,128)S(1)}, f32[10,2048]{1,0:T(8,128)}, u32[]{:S(2)}) copy-start(f32[10,2048]{1,0:T(8,128)} %param.18) | copy-start | bytes 245764
  149.3 41.4 %copy-start.7 = (f32[1,2048]{1,0:T(1,128)S(1)}, f32[1,2048]{1,0:T(1,128)}, u32[]{:S(2)}) copy-start(f32[1,2048]{1,0:T(1,128)} %param.15) | copy-start | bytes 24580
Sparse Core Ops, SparseCore 0:
  161.1 29.6 all-reduce.7
where the time goes:
time: 200 us; the launch traced here: 199 us
  local copies, waits for them, and re-layouts  62.6 us (31%)
  waiting for transfers between devices  37.7 us (19%)
  other arithmetic  29 us (14%)
  matrix products  20.8 us (10%)
  blocking collectives  20.6 us (10%)
  between operations  14.6 us (7%)
  starting transfers between devices  14.1 us (7%)
    slice x1, local copies, waits for them, and re-layouts, project(): cams[:, 1, 3]  36.3 us
    psum x1, waiting for transfers between devices, body(): gradient = lax.psum(gradient, 'depth')  23.9 us
    dot_general x4, matrix products, running_sum(): jnp.einsum('pbk,kj->pbj', blocks, triangle, precision=lax.Precision.HIGHEST)  17.8 us
    scatter-add x1, other arithmetic, body(): gradient = jnp.zeros_like(params).at[:, rows_in].add(slot_grad)  9.18 us
    all_to_all x1, blocking collectives, body(): lax.all_to_all(outgoing, 'tile', split_axis=1, concat_axis=1, tiled=True)  9.17 us
    all_to_all x1, starting transfers between devices, body(): lax.all_to_all(request, 'tile', split_axis=1, concat_axis=1, tiled=True)  7.31 us
    gather x3, local copies, waits for them, and re-layouts, body(): screen = project(params[:, rows_in], cameras[views_in])  6.92 us
    all_to_all x1, blocking collectives, body(): lax.all_to_all(own_grad, 'depth', split_axis=2, concat_axis=0, tiled=True)  6.22 us
  transfers between devices with their start and end apart: 4, of which 4 were waited for; matrix products, arithmetic and copies ran while one was open for 2% of the time, Pallas kernels for 0%

commit v1 on v0

--- a/solution.py
+++ b/solution.py
@@ -183,7 +183,7 @@
     unused, pullback = jax.vjp(lambda chosen: project(chosen, chosen_cams), params[:, rows_in])
     (slot_grad,) = pullback(incoming.reshape(9, -1))
     gradient = jnp.zeros_like(params).at[:, rows_in].add(slot_grad)
-    gradient = lax.psum(gradient, "depth")
+    gradient = jnp.sum(lax.all_gather(gradient, "depth"), axis=0)
     new_params, new_first, new_second = adam_update(params, first_moment, second_moment, gradient)
     return (image, new_params, new_first, new_second)
 

time: 200 us -> 165 us (0.82)
  waiting for transfers between devices: 37.7 us -> 14.7 us
  between operations: 14.6 us -> 1.23 us
  starting transfers between devices: 14.1 us -> 17.4 us
  blocking collectives: 20.6 us -> 18 us
    psum x1 -> x0, waiting for transfers between devices: 23.9 us -> none  [body(): gradient = lax.psum(gradient, 'depth')]
    all_to_all x1 -> x0, blocking collectives: 9.17 us -> none  [body(): lax.all_to_all(outgoing, 'tile', split_axis=1, concat_axis=1, tiled=True)]
    all_gather x0 -> x1, blocking collectives: none -> 6.5 us  [body(): gradient = jnp.sum(lax.all_gather(gradient, 'depth'), axis=0)]
    all_to_all x0 -> x1, starting transfers between devices: none -> 3.35 us  [body(): lax.all_to_all(outgoing, 'tile', split_axis=1, concat_axis=1, tiled=True)]
    unnamed x29 -> x30, local copies, waits for them, and re-layouts: 4.01 us -> 4.97 us
where the time goes in v1:
time: 165 us; the launch traced here: 163 us
  local copies, waits for them, and re-layouts  62.5 us (38%)
  other arithmetic  28.4 us (17%)
  matrix products  20.9 us (13%)
  blocking collectives  18 us (11%)
  starting transfers between devices  17.4 us (11%)
  waiting for transfers between devices  14.7 us (9%)
    slice x1, local copies, waits for them, and re-layouts, project(): cams[:, 1, 3]  36.3 us
    dot_general x4, matrix products, running_sum(): jnp.einsum('pbk,kj->pbj', blocks, triangle, precision=lax.Precision.HIGHEST)  17.9 us
    scatter-add x1, other arithmetic, body(): gradient = jnp.zeros_like(params).at[:, rows_in].add(slot_grad)  9.18 us
    all_to_all x1, starting transfers between devices, body(): lax.all_to_all(request, 'tile', split_axis=1, concat_axis=1, tiled=True)  7.31 us
    gather x3, local copies, waits for them, and re-layouts, body(): screen = project(params[:, rows_in], cameras[views_in])  6.92 us
    all_gather x1, blocking collectives, body(): gradient = jnp.sum(lax.all_gather(gradient, 'depth'), axis=0)  6.5 us
    all_to_all x1, blocking collectives, body(): lax.all_to_all(own_grad, 'depth', split_axis=2, concat_axis=0, tiled=True)  6.22 us
    all_to_all x1, waiting for transfers between devices, body(): lax.all_to_all(screen, 'tile', split_axis=1, concat_axis=1, tiled=True)  5.89 us
  transfers between devices with their start and end apart: 4, of which 4 were waited for; matrix products, arithmetic and copies ran while one was open for 2% of the time, Pallas kernels for 0%

profile of v1, /device:TPU:0, one launch (start us, length us, event | category | flops | bytes accessed | tf_op | source)
XLA Modules:
  0.0 163.1 jit_solution(17925172641896074273)
XLA Ops:
  1.4 1.1 reduce-window.6
  5.8 1.9 %scatter_custom_fusion = s32[2,1280]{0,1:T(8,128)S(1)} fusion(s32[512]{0:T(512)S(1)} %bitcast.199, s32[512,2]{1,0:T(8,128)S(1)} %copy.137, s32[]{:T(128)} %constant.127.clone.1), kind=kCustom, calls=%fused_computation.77 | custom fusion | bytes 10244 | tf_op jit(solution)/shard_map/scatter | solution.py:101
  7.7 0.9 copy.138
  8.6 7.3 %all-to-all-start = ((s32[2,8,160]{2,0,1:T(2,128)}), s32[2,8,160]{2,0,1:T(2,128)S(1)}, u32[]{:S(2)}, u32[]{:S(2)}) async-start(s32[2,8,160]{2,0,1:T(2,128)} %copy.138), calls=%async_computation | async-start | bytes 32768 | tf_op jit(solution)/shard_map/all_to_all | solution.py:104
  16.0 0.9 pad_maximum_fusion
  17.8 4.7 %all-to-all-done = s32[2,8,160]{2,0,1:T(2,128)S(1)} async-done(((s32[2,8,160]{2,0,1:T(2,128)}), s32[2,8,160]{2,0,1:T(2,128)S(1)}, u32[]{:S(2)}, u32[]{:S(2)}) %all-to-all-start) | async-done | bytes 10272 | tf_op jit(solution)/shard_map/all_to_all | solution.py:104
  22.7 4.3 %gather_fusion = f32[1280,2,4]{2,1,0:T(2,128)S(1)} fusion(f32[4,2,4]{2,1,0:T(2,128)S(1)} %copy-done.1, s32[2048]{0:T(1024)S(1)} %pad_clamp_fusion.1), kind=kCustom, calls=%fused_computation | custom fusion | bytes 87040 | tf_op jit(solution)/shard_map/gather | solution.py:107
  27.0 1.8 %fusion.84 = (f32[1280,1,3]{2,1,0:T(1,128)S(1)}, f32[1280,1,3]{2,1,0:T(1,128)}) fusion(f32[1280,2,4]{2,1,0:T(2,128)S(1)} %gather_fusion), kind=kLoop, calls=%fused_computation.179 | loop fusion | bytes 61440 | tf_op jit(solution)/shard_map/slice | solution.py:13
  28.8 36.3 %slice_reduce_fusion = (f32[1280]{0:T(1024)S(1)}, f32[1280]{0:T(1024)S(1)}) fusion(f32[1280,2,4]{2,1,0:T(2,128)S(1)} %gather_fusion), kind=kLoop, calls=%fused_computation.71 | loop fusion | bytes 20480 | tf_op jit(solution)/shard_map/slice | solution.py:15
  65.1 1.3 copy.175
  66.9 2.4 %gather_fusion.1 = f32[1280,10]{1,0:T(8,128)S(1)} fusion(f32[10,2048]{0,1:T(8,128)S(1)} %copy.140, s32[2048]{0:T(1024)S(1)} %pad_clamp_fusion), kind=kCustom, calls=%fused_computation.1 | custom fusion | bytes 107520 | tf_op jit(solution)/shard_map/gather | solution.py:107
  71.5 3.5 %all-to-all-start.1 = ((f32[8,1,1440]{2,1,0:T(1,128)}), f32[8,1,1440]{2,1,0:T(1,128)S(1)}, u32[]{:S(2)}, u32[]{:S(2)}) async-start(f32[8,1,1440]{2,1,0:T(1,128)} %reshape.1456), calls=%async_computation.1 | async-start | bytes 98304 | tf_op jit(solution)/shard_map/all_to_all | solution.py:109
  75.7 5.9 %all-to-all-done.1 = f32[8,1,1440]{2,1,0:T(1,128)S(1)} async-done(((f32[8,1,1440]{2,1,0:T(1,128)}), f32[8,1,1440]{2,1,0:T(1,128)S(1)}, u32[]{:S(2)}, u32[]{:S(2)}) %all-to-all-start.1) | async-done | bytes 46112 | tf_op jit(solution)/shard_map/all_to_all | solution.py:109
  83.2 1.0 gather_fusion.2
  85.0 3.3 %all-to-all-start.2 = ((f32[4,9,128]{2,1,0:T(8,128)}), f32[4,9,128]{2,1,0:T(8,128)S(1)}, u32[]{:S(2)}, u32[]{:S(2)}) async-start(f32[4,9,128]{2,1,0:T(8,128)} %bitcast.21), calls=%async_computation.2 | async-start | bytes 65536 | tf_op jit(solution)/shard_map/all_to_all | solution.py:161
  88.9 3.3 %all-to-all-done.2 = f32[4,9,128]{2,1,0:T(8,128)S(1)} async-done(((f32[4,9,128]{2,1,0:T(8,128)}), f32[4,9,128]{2,1,0:T(8,128)S(1)}, u32[]{:S(2)}, u32[]{:S(2)}) %all-to-all-start.2) | async-done | bytes 18464 | tf_op jit(solution)/shard_map/all_to_all | solution.py:161
  92.2 2.0 %fusion.28 = f32[1024,4]{0,1:T(4,128)S(1)} fusion(f32[4,128]{1,0:T(4,128)S(1)} %fusion.74, f32[4,128]{1,0:T(4,128)S(1)} %bitcast.167, f32[4,128]{1,0:T(4,128)S(1)} %bitcast.172, f32[1024]{0:T(1024)S(1)} %get-tuple-element.136, f32[4,128]{1,0:T(4,128)S(1)} %broadcast_multiply_fusion.1, f32[4,128]{1,0:T(4,128)S(1)} %bitcast.177, ...), kind=kLoop, calls=%fused_computation.63 | loop fusion | flops 7860224 | bytes 38912 | tf_op jit(solution)/shard_map/while/body/eval_jaxpr/reduce_sum | solution.py:56
  94.2 5.9 %multiply_reduce_fusion.3 = (f32[1024,4]{0,1:T(4,128)S(1)}, f32[1024,4]{0,1:T(4,128)S(1)}, f32[1024,4]{0,1:T(4,128)S(1)}, f32[1024,4,128]{0,2,1:T(8,128)S(1)}, f32[1024,4,128]{0,2,1:T(8,128)}) fusion(f32[4,128]{1,0:T(4,128)S(1)} %bitcast.210, f32[4,128]{1,0:T(4,128)S(1)} %bitcast.190, f32[4,128]{1,0:T(4,128)S(1)} %bitcast.187, f32[1024,4]{0,1:T(4,128)S(1)} %sub.316, ...), kind=kOutput, calls=%fused_computation.60 | convolution fusion | flops 823660544 | bytes 4288512 | tf_op jit(solution)/shard_map/while/body/eval_jaxpr/pbk,kj->pbj/dot_general | solution.py:55
  100.1 2.9 %fusion.24 = f32[1024,4,128]{0,2,1:T(8,128)} fusion(f32[1024,4,128]{0,2,1:T(8,128)S(1)} %get-tuple-element.96, f32[4,128]{1,0:T(4,128)S(1)} %bitcast.191), kind=kOutput, calls=%fused_computation.58 | convolution fusion | flops 805847040 | bytes 4196352 | tf_op jit(solution)/shard_map/while/body/eval_jaxpr/pbk,kj->pbj/dot_general | solution.py:55
  103.0 2.9 %fusion.22 = f32[1024,4,128]{0,2,1:T(8,128)} fusion(f32[1024,4,128]{0,2,1:T(8,128)S(1)} %get-tuple-element.96, f32[4,128]{1,0:T(4,128)S(1)} %bitcast.188), kind=kOutput, calls=%fused_computation.55 | convolution fusion | flops 805847040 | bytes 4196352 | tf_op jit(solution)/shard_map/while/body/eval_jaxpr/pbk,kj->pbj/dot_general | solution.py:55
  105.9 1.9 %fusion.14 = f32[1024]{0:T(1024)S(1)} fusion(f32[512]{0:T(512)S(1)} %fusion.75, f32[512]{0:T(512)S(1)} %bitcast.169, f32[512]{0:T(512)S(1)} %bitcast.174, f32[1024]{0:T(1024)S(1)} %get-tuple-element.136, f32[512]{0:T(512)S(1)} %bitcast.216, f32[512]{0:T(512)S(1)} %bitcast.179, f32[1024]{0:T(1024)S(1)} %get-tuple-element.135, f32[512]{0:T(512)S(1)} %bitcast.184, ...), kind=kLoop, calls=%fused_computation.40 | loop fusion | flops 7863296 | bytes 26624 | tf_op jit(solution)/shard_map/while/body/eval_jaxpr/reduce_sum | solution.py:122
  107.8 1.1 copy_subtract_fusion
  108.9 1.8 %fusion.56 = f32[3,512]{1,0:T(4,128)S(1)} fusion(f32[1024,512]{0,1:T(8,128)S(1)} %bitcast.143, f32[1,3,1024]{2,1,0:T(4,128)S(1)} %get-tuple-element.129), kind=kOutput, calls=%fused_computation.112 | convolution fusion | flops 18874368 | bytes 2115584 | tf_op jit(solution)/shard_map/while/body/eval_jaxpr/cp,pk->ck/dot_general | solution.py:140
  111.0 6.3 %multiply_multiply_fusion = (f32[1024,4,128]{0,2,1:T(8,128)S(1)}, f32[1024,4,128]{0,2,1:T(8,128)S(1)}) fusion(f32[4,128]{1,0:T(4,128)S(1)} %fusion.74, f32[4,128]{1,0:T(4,128)S(1)} %bitcast.170, f32[4,128]{1,0:T(4,128)S(1)} %bitcast.175, f32[1024]{0:T(1024)S(1)} %get-tuple-element.136, f32[4,128]{1,0:T(4,128)S(1)} %broadcast_multiply_fusion.1, ...), kind=kOutput, calls=%fused_computation.49 | convolution fusion | flops 825245696 | bytes 12701696 | tf_op jit(solution)/shard_map/while/body/eval_jaxpr/pbk,kj->pbj/dot_general | solution.py:55
  117.3 4.1 %fusion.3 = (f32[4,128]{1,0:T(4,128)S(1)}, f32[4,128]{1,0:T(4,128)S(1)}, f32[4,128]{1,0:T(4,128)S(1)}, f32[4,128]{1,0:T(4,128)S(1)}, f32[4,128]{1,0:T(4,128)S(1)}, /*index=5*/f32[4,128]{1,0:T(4,128)S(1)}) fusion(f32[1024,4,128]{0,2,1:T(8,128)S(1)} %get-tuple-element.131, f32[4,128]{1,0:T(4,128)S(1)} %bitcast.164, f32[4,128]{1,0:T(4,128)S(1)} %bitcast.171, ...), kind=kLoop, calls=%fused_computation.29 | loop fusion | flops 17298432 | bytes 4229120 | tf_op jit(solution)/shard_map/while/body/eval_jaxpr/reduce_sum | solution.py:146
  121.7 1.3 reduce.42
  123.2 6.2 %all_to_all.48 = f32[4,1,1152]{2,1,0:T(1,128)S(1)} all-to-all(f32[4,1,1152]{2,1,0:T(1,128)S(1)} %reshape.1458), channel_id=1, replica_groups=mesh['tile'=8,'depth'=4] {'depth'}, dimensions={0} | all-to-all | bytes 36864 | tf_op jit(solution)/shard_map/all_to_all | solution.py:174
  130.8 1.9 %scatter_custom_fusion.1 = f32[9,1280]{0,1:T(8,128)S(1)} fusion(s32[512]{0:T(512)S(1)} %bitcast.201, f32[512,9]{1,0:T(8,128)S(1)} %bitcast.158, f32[]{:T(128)} %constant.132.clone.1), kind=kCustom, calls=%fused_computation.75 | custom fusion | bytes 46084 | tf_op jit(solution)/shard_map/scatter | solution.py:177
  133.8 3.3 %all-to-all-start.4 = ((f32[8,1,1440]{2,1,0:T(1,128)}), f32[8,1,1440]{2,1,0:T(1,128)S(1)}, u32[]{:S(2)}, u32[]{:S(2)}) async-start(f32[8,1,1440]{2,1,0:T(1,128)} %reshape.1460), calls=%async_computation.4 | async-start | bytes 98304 | tf_op jit(solution)/shard_map/all_to_all | solution.py:179
  137.2 5.2 %all-gather.2 = f32[4,3,1024]{2,1,0:T(4,128)S(1)} all-gather(f32[1,3,1024]{2,1,0:T(4,128)S(1)} %get-tuple-element.130), channel_id=2, replica_groups=mesh['tile'=8,'depth'=4] {'depth'}, dimensions={0}, use_global_device_ids=true | all-gather | bytes 61440 | tf_op jit(solution)/shard_map/all_gather | solution.py:175
  146.2 9.2 %scatter_custom_fusion.2 = f32[10,2048]{0,1:T(8,128)S(1)} fusion(s32[1280]{0:T(1024)S(1)} %fusion.60, f32[1280,10]{1,0:T(8,128)S(1)} %copy.164, f32[]{:T(128)} %constant.132.clone.1), kind=kCustom, calls=%fused_computation.73 | custom fusion | flops 12800 | bytes 81924 | tf_op jit(solution)/shard_map/scatter-add | solution.py:185
  155.7 6.5 %all-gather.3 = f32[4,10,2048]{2,1,0:T(8,128)S(1)} all-gather(f32[1,10,2048]{2,1,0:T(8,128)S(1)} %copy.165), channel_id=3, replica_groups=mesh['tile'=8,'depth'=4] {'depth'}, dimensions={0}, use_global_device_ids=true | all-gather | bytes 409600 | tf_op jit(solution)/shard_map/all_gather | solution.py:186
  (119 shorter events, 19.6 us)
Async XLA Ops:
  0.6 15.3 %copy-start = (f32[4,3,1024]{2,0,1:T(4,128)S(1)}, f32[4,3,1024]{2,0,1:T(4,128)}, u32[]{:S(2)}) copy-start(f32[4,3,1024]{2,0,1:T(4,128)} %param.21) | copy-start | bytes 147460
  0.6 16.6 %copy-start.9 = (s32[4]{0:T(128)S(1)}, s32[4]{0:T(128)}, u32[]{:S(2)}) copy-start(s32[4]{0:T(128)} %param.23) | copy-start | bytes 52
  0.7 22.0 %copy-start.1 = (f32[4,2,4]{2,1,0:T(2,128)S(1)}, f32[4,2,4]{2,1,0:T(2,128)}, u32[]{:S(2)}) copy-start(f32[4,2,4]{2,1,0:T(2,128)} %param.19) | copy-start | bytes 388
  8.6 13.9 %all-to-all-start = ((s32[2,8,160]{2,0,1:T(2,128)}), s32[2,8,160]{2,0,1:T(2,128)S(1)}, u32[]{:S(2)}, u32[]{:S(2)}) async-start(s32[2,8,160]{2,0,1:T(2,128)} %copy.138), calls=%async_computation | async-start | bytes 32768 | tf_op jit(solution)/shard_map/all_to_all | solution.py:104
  71.5 10.1 %all-to-all-start.1 = ((f32[8,1,1440]{2,1,0:T(1,128)}), f32[8,1,1440]{2,1,0:T(1,128)S(1)}, u32[]{:S(2)}, u32[]{:S(2)}) async-start(f32[8,1,1440]{2,1,0:T(1,128)} %reshape.1456), calls=%async_computation.1 | async-start | bytes 98304 | tf_op jit(solution)/shard_map/all_to_all | solution.py:109
  85.0 7.2 %all-to-all-start.2 = ((f32[4,9,128]{2,1,0:T(8,128)}), f32[4,9,128]{2,1,0:T(8,128)S(1)}, u32[]{:S(2)}, u32[]{:S(2)}) async-start(f32[4,9,128]{2,1,0:T(8,128)} %bitcast.21), calls=%async_computation.2 | async-start | bytes 65536 | tf_op jit(solution)/shard_map/all_to_all | solution.py:161
  103.0 4.8 %copy-start.8 = (f32[3]{0:T(128)S(1)}, f32[3]{0:T(128)}, u32[]{:S(2)}) copy-start(f32[3]{0:T(128)} %param.20) | copy-start | bytes 40
  133.8 10.1 %all-to-all-start.4 = ((f32[8,1,1440]{2,1,0:T(1,128)}), f32[8,1,1440]{2,1,0:T(1,128)S(1)}, u32[]{:S(2)}, u32[]{:S(2)}) async-start(f32[8,1,1440]{2,1,0:T(1,128)} %reshape.1460), calls=%async_computation.4 | async-start | bytes 98304 | tf_op jit(solution)/shard_map/all_to_all | solution.py:179
  145.8 16.4 %copy-start.2 = (f32[3,2048]{1,0:T(4,128)S(1)}, f32[3,2048]{1,0:T(4,128)}, u32[]{:S(2)}) copy-start(f32[3,2048]{1,0:T(4,128)} %param.16) | copy-start | bytes 73732
  145.8 16.4 %copy-start.3 = (f32[3,2048]{1,0:T(4,128)S(1)}, f32[3,2048]{1,0:T(4,128)}, u32[]{:S(2)}) copy-start(f32[3,2048]{1,0:T(4,128)} %param.14) | copy-start | bytes 73732
  145.8 16.4 %copy-start.4 = (f32[3,2048]{1,0:T(4,128)S(1)}, f32[3,2048]{1,0:T(4,128)}, u32[]{:S(2)}) copy-start(f32[3,2048]{1,0:T(4,128)} %param.13) | copy-start | bytes 73732
  145.9 16.4 %copy-start.5 = (f32[10,2048]{1,0:T(8,128)S(1)}, f32[10,2048]{1,0:T(8,128)}, u32[]{:S(2)}) copy-start(f32[10,2048]{1,0:T(8,128)} %param.17) | copy-start | bytes 245764
  145.9 16.4 %copy-start.6 = (f32[10,2048]{1,0:T(8,128)S(1)}, f32[10,2048]{1,0:T(8,128)}, u32[]{:S(2)}) copy-start(f32[10,2048]{1,0:T(8,128)} %param.18) | copy-start | bytes 245764
  145.9 16.4 %copy-start.7 = (f32[1,2048]{1,0:T(1,128)S(1)}, f32[1,2048]{1,0:T(1,128)}, u32[]{:S(2)}) copy-start(f32[1,2048]{1,0:T(1,128)} %param.15) | copy-start | bytes 24580
